TPU v7x, 128 devices: a whole 4x4x4 slice. The times are simulated.
128 devices in a mesh: span: 8 (over x, y_lo), tok: 16 (over z, y_hi, core).
Axes of the slice: x: 4, y: 4 (y_hi: 2, y_lo: 2; y = y_hi * 2 + y_lo), z: 4, core: 2. Of those that a mesh axis runs over, the one named last changes fastest.
Arguments:
- latents: bfloat16 [8, 1024, 3584], P('span', 'tok'), may hold values from -6 to 6
- levels: int32 [8], P('span'), may hold values from 0 to 14
- visible: int32 [8, 8], replicated, may hold values 0 or 1
- frame_counts: int32 [8], replicated, may hold values from 0 to 2
- modulation: float32 [16, 3, 3584], replicated, may hold values from -4 to 4
- w_qkv: bfloat16 [3584, 3, 4096], P(None, None, 'tok')
- qk_gain: float32 [2, 4096], P(None, 'tok'), may hold values from 0 to 5
- w_out: bfloat16 [4096, 3584], P('tok'), may hold values from -0.09375 to 0.09375
- w_head: bfloat16 [3584, 96], replicated, may hold values from -0.09375 to 0.09375
- conv_w: bfloat16 [3, 96, 384], replicated, may hold values from -0.375 to 0.375
Outputs:
- denoised: bfloat16 [8, 1024, 3584], P('span', 'tok')
- decoded: bfloat16 [8, 1024, 384], P('span', 'tok')
All inputs are finite; a program needn't handle non-finite values.
Results may differ from a plain program's by a relative error of at most 0.015.
Values may be sent and summed in bfloat16 or wider, within the bound.
A program may use at most 128 MiB of HBM per device.

v0:
```python
import jax
import jax.numpy as jnp
from jax import lax
from jax.sharding import PartitionSpec as P

HD = 128
FRAMES = 8
KEEP = 2
SPOTS = 8
TOK_DEV = 64
EPS = 1e-06
NEG = -1e30


def from_behind(array, axis, by):
    devices = lax.axis_size(axis)
    pairs = [(i, i + by) for i in range(devices) if 0 <= i + by < devices]
    return lax.ppermute(array, axis, pairs)


def modulate(rows, shift, scale):
    values = rows.astype(jnp.float32)
    centre = values - jnp.mean(values, -1, keepdims=True)
    spread = jnp.mean(centre * centre, -1, keepdims=True)
    return (centre * lax.rsqrt(spread + EPS) * (1.0 + scale) + shift).astype(jnp.bfloat16)


def qk_scale(tensor, gain):
    square = jnp.mean(tensor * tensor, -1, keepdims=True)
    return (
        tensor * lax.rsqrt(square + EPS) * gain.reshape(tensor.shape[-2], tensor.shape[-1])
    ).astype(jnp.bfloat16)


def pick_level(table, level):
    matched = jnp.arange(table.shape[0]) == level
    picked = jnp.sum(jnp.where(matched[:, None, None], table, 0.0), 0)
    return (picked[0], picked[1], picked[2])


def lookup_one(table, index):
    matched = jnp.arange(table.shape[0], dtype=jnp.int32) == index
    return jnp.sum(jnp.where(matched, table, 0))


def fold_block(carry, query, block_keys, block_values, allow):
    best, total, acc = carry
    scores = jnp.einsum(
        "qhd,khd->hqk", query, block_keys, preferred_element_type=jnp.float32
    ) * HD ** (-0.5)
    scores = jnp.where(allow[None, None, :], scores, NEG)
    fresh = jnp.maximum(best, jnp.max(scores, -1))
    terms = jnp.where(allow[None, None, :], jnp.exp(scores - fresh[..., None]), 0.0)
    decay = jnp.exp(best - fresh)
    total = total * decay + jnp.sum(terms, -1)
    acc = acc * decay[..., None] + jnp.einsum(
        "hqk,khd->hqd", terms.astype(jnp.bfloat16), block_values, preferred_element_type=jnp.float32
    )
    return (fresh, total, acc)


def attention(proj, qk_gain, clip_id, visible_row, frame_counts):
    rows = proj.shape[0]
    cols = qk_gain.shape[1]
    heads = cols // HD
    tiles = rows // TOK_DEV
    lead = KEEP * SPOTS
    split = proj.reshape(rows, 3, heads, HD)
    query = qk_scale(split[:, 0], qk_gain[0])
    keys = qk_scale(split[:, 1], qk_gain[1])
    values = split[:, 2].astype(jnp.bfloat16)
    start_carry = (
        jnp.full((heads, rows), NEG, jnp.float32),
        jnp.zeros((heads, rows), jnp.float32),
        jnp.zeros((heads, rows, HD), jnp.float32),
    )
    everywhere = jnp.ones((rows,), jnp.bool_)
    own = fold_block(start_carry, query, keys, values, everywhere)
    lead_keys = keys.reshape(tiles, TOK_DEV, cols)[:, :lead].reshape(tiles * lead, cols)
    lead_values = values.reshape(tiles, TOK_DEV, cols)[:, :lead].reshape(tiles * lead, cols)
    packed = jnp.stack([lead_keys, lead_values], 0)[None]
    count = tiles * lead
    frame = jnp.arange(count, dtype=jnp.int32) % lead // SPOTS
    carry = own
    piece = lax.all_gather(packed, "span", axis=0, tiled=True)
    start = jnp.int32(0)
    for index in range(piece.shape[0]):
        source = start + index
        seen = lookup_one(visible_row, source)
        limit = lookup_one(frame_counts, source)
        allow = (frame < limit) & (source < clip_id) & (seen == 1)
        block_keys = piece[index, 0].reshape(count, heads, HD)
        block_values = piece[index, 1].reshape(count, heads, HD)
        carry = fold_block(carry, query, block_keys, block_values, allow)
    best, total, acc = carry
    return (acc / total[..., None]).transpose(1, 0, 2).reshape(rows, cols).astype(jnp.bfloat16)


def head_terms(attended, w_out):
    partial_term = jnp.dot(attended, w_out, preferred_element_type=jnp.float32).astype(jnp.bfloat16)
    return lax.optimization_barrier(partial_term).astype(jnp.float32)


def per_device(
    latents, levels, visible, frame_counts, modulation, w_qkv, qk_gain, w_out, w_head, conv_w
):
    current = latents[0]
    tok_rows = current.shape[0]
    width = current.shape[1]
    clip_id = lax.axis_index("span")
    level = levels[0]
    visible_row = lax.dynamic_index_in_dim(visible, clip_id, 0, keepdims=False)
    w_flat = w_qkv.reshape(width, -1)
    shift, scale, gate = pick_level(modulation, level)
    modulated = modulate(current, shift, scale)
    proj = jnp.dot(
        lax.all_gather(modulated, "tok", axis=0, tiled=True),
        w_flat,
        preferred_element_type=jnp.float32,
    )
    attended = attention(proj, qk_gain, clip_id, visible_row, frame_counts)
    summed = lax.psum_scatter(
        head_terms(attended, w_out).astype(jnp.bfloat16), "tok", scatter_dimension=0, tiled=True
    ).astype(jnp.float32)
    current = (current.astype(jnp.float32) + gate * summed).astype(jnp.bfloat16)
    channels = w_head.shape[1]
    feats = jnp.dot(current, w_head, preferred_element_type=jnp.float32).astype(jnp.bfloat16)
    feats = feats.reshape(FRAMES, tok_rows // FRAMES, channels)
    earlier = from_behind(feats[FRAMES - 2 :], "span", 1)
    sequence = jnp.concatenate([earlier, feats], 0)
    conv = jnp.zeros((tok_rows, conv_w.shape[2]), jnp.float32)
    for tap in range(3):
        window = sequence[2 - tap : 2 - tap + FRAMES].reshape(tok_rows, channels)
        conv = conv + jnp.dot(window, conv_w[tap], preferred_element_type=jnp.float32)
    decoded = jax.nn.silu(conv).astype(jnp.bfloat16)
    return (current[None], decoded[None])


def solution(mesh):
    placed = (
        P("span", "tok", None),
        P("span"),
        P(),
        P(),
        P(),
        P(None, None, "tok"),
        P(None, "tok"),
        P("tok", None),
        P(),
        P(),
    )
    return jax.shard_map(
        per_device,
        mesh=mesh,
        in_specs=placed,
        out_specs=(P("span", "tok", None), P("span", "tok", None)),
        check_vma=False,
    )
```

profile of v0, /device:TPU:2, one launch (start us, length us, event | category | flops | bytes accessed | tf_op | source)
XLA Modules:
  0.0 300.7 jit_solution(5046137200241144354)
XLA Ops:
  8.0 1.2 convert_reduce_fusion
  9.2 1.3 fusion.113
  10.5 1.3 select_reduce_fusion
  12.0 2.0 fusion.116
  14.1 8.3 %copy.78 = bf16[3584,3,256]{0,2,1:T(8,128)(2,1)} copy(bf16[3584,3,256]{2,0,1:T(8,128)(2,1)} %param.15) | data formatting | bytes 11010048 | tf_op args[5]
  22.4 0.6 fusion.203
  23.0 61.9 %all-gather.4.cloned.1.call-done = bf16[1024,3584]{1,0:T(8,128)(2,1)} async-done(((bf16[64,3584]{1,0:T(8,128)(2,1)}), bf16[1024,3584]{1,0:T(8,128)(2,1)}) %all-gather.4.cloned.1.call-update) | async-done | bytes 7340048 | tf_op jit(solution)/shard_map/all_gather | solution.py:117
  84.9 9.8 %fusion = f32[1024,3,2,128]{0,3,2,1:T(8,128)S(1)} fusion(bf16[3,2,128,3584]{3,2,1,0:T(8,128)(2,1)} %bitcast.342, bf16[1024,3584]{1,0:T(8,128)(2,1)} %all-gather.4.cloned.1.call-done), kind=kOutput, calls=%fused_computation.3 | convolution fusion | flops 5637144576 | bytes 15990784 | tf_op jit(solution)/shard_map/dot_general | solution.py:116
  94.9 1.2 slice.205
  96.2 0.5 copy-done.1
  96.6 0.6 add_rsqrt_fusion
  97.8 2.0 mul.275.clone
  99.9 3.1 %mul.283 = f32[16,64,256]{2,1,0:T(8,128)} reshape(f32[1024,2,128]{2,1,0:T(2,128)} %mul.275.clone) | data formatting | bytes 2097152 | tf_op jit(solution)/shard_map/mul | solution.py:31
  103.0 1.3 copy.84
  104.3 1.1 convert_element_type.88
  105.5 1.3 copy.82
  106.8 2.1 squeeze.31
  108.9 1.0 fusion.124
  109.9 0.7 pad_maximum_fusion
  110.7 1.5 fusion.169
  117.3 0.7 fusion.168
  118.0 1.3 and_and_fusion
  119.3 1.3 and_and_fusion.2
  120.7 1.2 and_and_fusion.4
  121.9 1.1 and_and_fusion.6
  123.1 1.4 multiply_convert_fusion
  124.4 5.8 %multiply_reduce_fusion = (f32[2,1024]{1,0:T(2,128)S(1)}, f32[2,1024,1024]{1,2,0:T(8,128)}) fusion(bf16[1024,2,128]{0,2,1:T(8,128)(2,1)S(1)} %multiply_convert_fusion, f32[2,128]{1,0:T(2,128)S(1)} %bitcast.365, f32[1024,2]{0,1:T(2,128)S(1)} %copy-done.6, f32[1024,3,2,128]{0,3,2,1:T(8,128)} %copy-done.1), kind=kOutput, calls=%fused_computation.1 | convolution fusion | flops 541849600 | bytes 9978880 | tf_op jit(solution)/shard_map/qhd,khd->hqk/dot_general | solution.py:48
  130.2 28.9 %all-gather.6.cloned.1.call-done = bf16[16,256,256]{2,1,0:T(8,128)(2,1)} async-done(((bf16[2,256,256]{2,1,0:T(8,128)(2,1)}), bf16[16,256,256]{2,1,0:T(8,128)(2,1)}) %all-gather.6.cloned.1.call-update) | async-done | bytes 2097168 | tf_op jit(solution)/shard_map/all_gather | solution.py:85
  159.1 3.9 %copy.85 = bf16[16,256,256]{1,2,0:T(8,128)(2,1)} copy(bf16[16,256,256]{2,1,0:T(8,128)(2,1)} %all-gather.6.cloned.1.call-done) | data formatting | bytes 4194304 | tf_op jit(solution)/shard_map/all_gather | solution.py:85
  163.0 1.7 fusion.202
  164.8 0.5 fusion.15
  165.3 0.5 fusion.14
  165.8 0.5 fusion.13
  166.3 0.5 fusion.12
  166.9 0.5 fusion.11
  167.4 0.5 fusion.10
  167.9 0.5 fusion.9
  168.5 0.5 fusion.8
  169.1 0.6 fusion.30
  169.7 0.6 fusion.28
  170.4 0.6 fusion.26
  171.0 0.6 fusion.24
  171.7 0.6 fusion.22
  172.3 0.6 fusion.20
  172.9 0.6 fusion.18
  173.6 0.6 fusion.16
  174.2 1.4 fusion.2
  175.7 0.4 copy-done.2
  176.1 2.0 fusion.54
  178.1 0.7 fusion.50
  178.9 0.7 fusion.48
  179.6 0.7 fusion.46
  180.3 0.7 fusion.44
  181.1 0.7 fusion.42
  181.8 0.7 fusion.40
  182.6 0.7 fusion.38
  183.3 0.7 fusion.57
  184.1 5.1 %convolution_convert_fusion = bf16[1024,3584]{1,0:T(8,128)(2,1)} fusion(bf16[1024,256]{0,1:T(8,128)(2,1)S(1)} %bitcast.343, bf16[256,3584]{1,0:T(8,128)(2,1)S(1)} %copy-done), kind=kOutput, calls=%fused_computation.2 | convolution fusion | flops 1882718208 | bytes 9699328 | tf_op jit(solution)/shard_map/dot_general | solution.py:100
  189.2 96.2 %reduce-scatter.2.cloned.1.call-done = bf16[64,3584]{1,0:T(8,128)(2,1)} async-done(((bf16[1024,3584]{1,0:T(8,128)(2,1)}), bf16[64,3584]{1,0:T(8,128)(2,1)}) %reduce-scatter.2.cloned.1.call-update) | async-done | bytes 458768 | tf_op jit(solution)/shard_map/reduce_scatter | solution.py:122
  285.4 1.4 convolution_convert_fusion.1
  286.8 2.5 collective-permute-start
  289.3 1.9 fusion.126
  291.4 1.9 collective-permute-done
  293.4 0.8 fusion.127
  (83 shorter events, 1.7 us)
Async XLA Ops:
  7.2 176.9 %copy-start = (bf16[256,3584]{1,0:T(8,128)(2,1)S(1)}, bf16[256,3584]{1,0:T(8,128)(2,1)}, u32[]{:S(2)}) copy-start(bf16[256,3584]{1,0:T(8,128)(2,1)} %param.17) | copy-start | bytes 5505028
  7.2 77.7 %all-gather.4.cloned.1.call-start = ((), (), s32[]{:S(2)}) async-start(), calls=%async_computation.1 | async-start | bytes 7798784 | tf_op jit(solution)/shard_map/all_gather | solution.py:117
  14.0 8.4 %copy-start.27 = (f32[2,256]{1,0:T(2,128)S(1)}, f32[2,256]{1,0:T(2,128)}, u32[]{:S(2)}) copy-start(f32[2,256]{1,0:T(2,128)} %param.16) | copy-start | bytes 6148
  14.0 145.1 %all-gather.6.cloned.1.call-start = ((), (), s32[]{:S(2)}) async-start(), calls=%async_computation.3 | async-start | bytes 2359296 | tf_op jit(solution)/shard_map/all_gather | solution.py:85
  94.7 1.9 copy-start.1
  97.3 0.6 copy-start.5
  99.9 5.6 %slice-start.2 = ((f32[1024,3,2,128]{0,3,2,1:T(8,128)}), f32[1024,1,2,128]{0,3,2,1:T(8,128)S(1)}, s32[]{:S(2)}) async-start(f32[1024,3,2,128]{0,3,2,1:T(8,128)} %copy-done.1), calls=%async_computation.6 | async-start | bytes 2097152 | tf_op jit(solution)/shard_map/slice | solution.py:70
  105.5 4.5 %slice-start.3 = ((bf16[16,64,256]{2,1,0:T(8,128)(2,1)}), bf16[16,16,256]{2,1,0:T(8,128)(2,1)S(1)}, s32[]{:S(2)}) async-start(bf16[16,64,256]{2,1,0:T(8,128)(2,1)} %convert_element_type.88), calls=%async_computation.7 | async-start | bytes 262144 | tf_op jit(solution)/shard_map/slice | solution.py:80
  106.8 2.1 copy-start.9
  106.8 10.5 %copy-start.28 = (s32[8]{0:T(128)S(1)}, s32[8]{0:T(128)}, u32[]{:S(2)}) copy-start(s32[8]{0:T(128)} %param.13) | copy-start | bytes 100
  106.8 16.2 %copy-start.8 = (f32[1024,2]{0,1:T(2,128)S(1)}, f32[1024,2]{0,1:T(2,128)}, u32[]{:S(2)}) copy-start(f32[1024,2]{0,1:T(2,128)} %get-tuple-element.81) | copy-start | bytes 24580
  106.8 16.3 %copy-start.26 = (f32[1,256]{1,0:T(1,128)S(1)}, f32[1,256]{1,0:T(1,128)}, u32[]{:S(2)}) copy-start(f32[1,256]{1,0:T(1,128)} %get-tuple-element.61) | copy-start | bytes 3076
  108.9 15.5 %copy-start.6 = (f32[1024,2]{0,1:T(2,128)S(1)}, f32[1024,2]{0,1:T(2,128)}, u32[]{:S(2)}) copy-start(f32[1024,2]{0,1:T(2,128)} %copy-done.5) | copy-start | bytes 24580
  110.7 174.7 %reduce-scatter.2.cloned.1.call-start = ((), (), s32[]{:S(2)}) async-start(), calls=%async_computation.2 | async-start | bytes 7798784 | tf_op jit(solution)/shard_map/reduce_scatter | solution.py:122
  119.3 49.8 %copy-start.10 = (pred[256]{0:T(512)(128)(4,1)}, pred[256]{0:T(512)(128)(4,1)S(1)}, u32[]{:S(2)}) copy-start(pred[256]{0:T(512)(128)(4,1)S(1)} %get-tuple-element.82) | copy-start | bytes 772
  119.3 50.4 %copy-start.12 = (pred[256]{0:T(512)(128)(4,1)}, pred[256]{0:T(512)(128)(4,1)S(1)}, u32[]{:S(2)}) copy-start(pred[256]{0:T(512)(128)(4,1)S(1)} %get-tuple-element.83) | copy-start | bytes 772
  120.6 49.7 %copy-start.14 = (pred[256]{0:T(512)(128)(4,1)}, pred[256]{0:T(512)(128)(4,1)S(1)}, u32[]{:S(2)}) copy-start(pred[256]{0:T(512)(128)(4,1)S(1)} %get-tuple-element.84) | copy-start | bytes 772
  120.6 50.3 %copy-start.16 = (pred[256]{0:T(512)(128)(4,1)}, pred[256]{0:T(512)(128)(4,1)S(1)}, u32[]{:S(2)}) copy-start(pred[256]{0:T(512)(128)(4,1)S(1)} %get-tuple-element.85) | copy-start | bytes 772
  121.8 45.0 %copy-start.18 = (pred[256]{0:T(512)(128)(4,1)}, pred[256]{0:T(512)(128)(4,1)S(1)}, u32[]{:S(2)}) copy-start(pred[256]{0:T(512)(128)(4,1)S(1)} %get-tuple-element.86) | copy-start | bytes 772
  121.9 45.6 %copy-start.20 = (pred[256]{0:T(512)(128)(4,1)}, pred[256]{0:T(512)(128)(4,1)S(1)}, u32[]{:S(2)}) copy-start(pred[256]{0:T(512)(128)(4,1)S(1)} %get-tuple-element.87) | copy-start | bytes 772
  123.0 44.9 %copy-start.22 = (pred[256]{0:T(512)(128)(4,1)}, pred[256]{0:T(512)(128)(4,1)S(1)}, u32[]{:S(2)}) copy-start(pred[256]{0:T(512)(128)(4,1)S(1)} %get-tuple-element.88) | copy-start | bytes 772
  123.0 45.5 %copy-start.24 = (pred[256]{0:T(512)(128)(4,1)}, pred[256]{0:T(512)(128)(4,1)S(1)}, u32[]{:S(2)}) copy-start(pred[256]{0:T(512)(128)(4,1)S(1)} %get-tuple-element.89) | copy-start | bytes 772
  169.1 5.1 %slice-start = ((s8[8388608]{0:T(1024)(128)(4,1)}), s8[4194304]{0:T(1024)(128)(4,1)S(1)}, s32[]{:S(2)}) async-start(s8[8388608]{0:T(1024)(128)(4,1)} %bitcast.339), calls=%async_computation.4 | async-start | bytes 8388608
  170.4 1.3 copy-start.19
  171.0 1.3 copy-start.21
  171.6 1.3 copy-start.23
  171.6 2.5 slice-start.1
  172.3 1.3 copy-start.25
  174.2 1.9 copy-start.2
  180.3 0.7 copy-start.17
  181.1 0.7 copy-start.15
  181.8 0.7 copy-start.13
  182.6 0.7 copy-start.11
  189.2 96.3 %copy-start.3 = (bf16[1,64,3584]{2,1,0:T(8,128)(2,1)S(1)}, bf16[1,64,3584]{2,1,0:T(8,128)(2,1)}, u32[]{:S(2)}) copy-start(bf16[1,64,3584]{2,1,0:T(8,128)(2,1)} %param.10) | copy-start | bytes 1376260
  189.2 96.3 %copy-start.4 = (bf16[3584,96]{0,1:T(8,128)(2,1)S(1)}, bf16[3584,96]{0,1:T(8,128)(2,1)}, u32[]{:S(2)}) copy-start(bf16[3584,96]{0,1:T(8,128)(2,1)} %param.18) | copy-start | bytes 2064388
  189.2 102.0 %copy-start.7 = (bf16[3,96,384]{2,1,0:T(8,128)(2,1)S(1)}, bf16[3,96,384]{2,1,0:T(8,128)(2,1)}, u32[]{:S(2)}) copy-start(bf16[3,96,384]{2,1,0:T(8,128)(2,1)} %param.19) | copy-start | bytes 663556
  286.8 6.4 %collective-permute-start = (bf16[2,8,96]{2,1,0:T(8,128)(2,1)S(1)}, bf16[2,8,96]{2,1,0:T(8,128)(2,1)S(1)}, u32[]{:S(2)}, u32[]{:S(2)}) collective-permute-start(bf16[2,8,96]{2,1,0:T(8,128)(2,1)S(1)} %slice_bitcast_fusion.1), channel_id=1, source_target_pairs={{0,16},{16,32},{32,48},{48,64},{64,80},{80,96},{96,112},{1,17},{17... | collective-permute-start | bytes 9224 | tf_op jit(solution)/shard_map/ppermute | solution.py:18
Sparse Core Ops, SparseCore 0:
  14.1 70.7 all-gather.3
  110.8 48.2 all-gather.5
  189.3 96.0 reduce-scatter.1
where the time goes:
time: 302 us; the launch traced here: 301 us
  waiting for transfers between devices  189 us (63%)
  matrix products  35.2 us (12%)
  local copies, waits for them, and re-layouts  28.4 us (9%)
  other arithmetic  25.4 us (8%)
  between operations  20.2 us (7%)
    reduce_scatter x1, waiting for transfers between devices, per_device(): lax.psum_scatter(head_terms(attended, w_out).astype(jnp.bfloat16), 'tok',...  96.2 us
    all_gather x1, waiting for transfers between devices, per_device(): lax.all_gather(modulated, 'tok', axis=0, tiled=True)  61.9 us
    all_gather x1, waiting for transfers between devices, attention(): piece = lax.all_gather(packed, 'span', axis=0, tiled=True)  28.9 us
    dot_general x9, matrix products, fold_block(): jnp.einsum('qhd,khd->hqk', query, block_keys, preferred_element_type=jnp....  9.99 us
    unnamed x64, local copies, waits for them, and re-layouts  9.9 us
    dot_general x1, matrix products, per_device(): jnp.dot(lax.all_gather(modulated, 'tok', axis=0, tiled=True), w_flat, pre...  9.76 us
    dot_general x9, matrix products, fold_block(): jnp.einsum('hqk,khd->hqd', terms.astype(jnp.bfloat16), block_values, pref...  7.87 us
    reduce_sum x9, other arithmetic, fold_block(): total = total * decay + jnp.sum(terms, -1)  6.35 us
  transfers between devices with their start and end apart: 4, of which 4 were waited for; matrix products, arithmetic and copies ran while one was open for 8% of the time, Pallas kernels for 0%

commit v1 on v0

--- a/solution.py
+++ b/solution.py
@@ -82,7 +82,9 @@
     count = tiles * lead
     frame = jnp.arange(count, dtype=jnp.int32) % lead // SPOTS
     carry = own
-    piece = lax.all_gather(packed, "span", axis=0, tiled=True)
+    piece = jnp.concatenate(
+        lax.all_to_all(jnp.stack([packed] * lax.axis_size("span")), "span", 0, 0), axis=0
+    )
     start = jnp.int32(0)
     for index in range(piece.shape[0]):
         source = start + index

time: 302 us -> 281 us (0.930)
  waiting for transfers between devices: 189 us -> 166 us
  starting transfers between devices: 2.59 us -> 7.49 us
    all_gather x1 -> x0, waiting for transfers between devices: 28.9 us -> none  [attention(): piece = lax.all_gather(packed, 'span', axis=0, tiled=True)]
    all_to_all x0 -> x1, waiting for transfers between devices: none -> 9.93 us  [attention(): lax.all_to_all(jnp.stack([packed] * lax.axis_size('span')), 'span', 0, 0)]
    all_to_all x0 -> x1, starting transfers between devices: none -> 4.97 us  [attention(): lax.all_to_all(jnp.stack([packed] * lax.axis_size('span')), 'span', 0, 0)]
    all_gather x1 -> x0, local copies, waits for them, and re-layouts: 3.92 us -> none  [attention(): piece = lax.all_gather(packed, 'span', axis=0, tiled=True)]
    reduce_scatter x1, waiting for transfers between devices: 96.2 us -> 92.5 us  [per_device(): lax.psum_scatter(head_terms(attended, w_out).astype(jnp.bfloat16), 'tok',...]
  transfers between devices with their start and end apart: 4 -> 4, of which waited for: 4 -> 4; matrix products, arithmetic and copies ran while one was open for 8% -> 9% of each run, Pallas kernels for 0% -> 0%
where the time goes in v1:
time: 281 us; the launch traced here: 280 us
  waiting for transfers between devices  166 us (59%)
  matrix products  34.9 us (12%)
  local copies, waits for them, and re-layouts  25.9 us (9%)
  other arithmetic  25.2 us (9%)
  between operations  20.4 us (7%)
  starting transfers between devices  7.49 us (3%)
    reduce_scatter x1, waiting for transfers between devices, per_device(): lax.psum_scatter(head_terms(attended, w_out).astype(jnp.bfloat16), 'tok',...  92.5 us
    all_gather x1, waiting for transfers between devices, per_device(): lax.all_gather(modulated, 'tok', axis=0, tiled=True)  62 us
    dot_general x9, matrix products, fold_block(): jnp.einsum('qhd,khd->hqk', query, block_keys, preferred_element_type=jnp....  9.98 us
    all_to_all x1, waiting for transfers between devices, attention(): lax.all_to_all(jnp.stack([packed] * lax.axis_size('span')), 'span', 0, 0)  9.93 us
    dot_general x1, matrix products, per_device(): jnp.dot(lax.all_gather(modulated, 'tok', axis=0, tiled=True), w_flat, pre...  9.76 us
    unnamed x64, local copies, waits for them, and re-layouts  9.69 us
    dot_general x9, matrix products, fold_block(): jnp.einsum('hqk,khd->hqd', terms.astype(jnp.bfloat16), block_values, pref...  7.65 us
    reduce_sum x9, other arithmetic, fold_block(): total = total * decay + jnp.sum(terms, -1)  6.56 us
  transfers between devices with their start and end apart: 4, of which 4 were waited for; matrix products, arithmetic and copies ran while one was open for 9% of the time, Pallas kernels for 0%

profile of v1, /device:TPU:2, one launch (start us, length us, event | category | flops | bytes accessed | tf_op | source)
XLA Modules:
  0.0 280.2 jit_solution(16193072567748462189)
XLA Ops:
  8.0 1.2 convert_reduce_fusion
  9.2 1.3 fusion.113
  10.5 1.3 select_reduce_fusion
  12.0 2.0 fusion.116
  14.0 8.3 %copy.63 = bf16[3584,3,256]{0,2,1:T(8,128)(2,1)} copy(bf16[3584,3,256]{2,0,1:T(8,128)(2,1)} %param.15) | data formatting | bytes 11010048 | tf_op args[5]
  22.3 0.6 fusion.203
  22.9 62.0 %all-gather.2.cloned.1.call-done = bf16[1024,3584]{1,0:T(8,128)(2,1)} async-done(((bf16[64,3584]{1,0:T(8,128)(2,1)}), bf16[1024,3584]{1,0:T(8,128)(2,1)}) %all-gather.2.cloned.1.call-update) | async-done | bytes 7340048 | tf_op jit(solution)/shard_map/all_gather | solution.py:119
  84.9 9.8 %fusion = f32[1024,3,2,128]{0,3,2,1:T(8,128)S(1)} fusion(bf16[3,2,128,3584]{3,2,1,0:T(8,128)(2,1)} %bitcast.341, bf16[1024,3584]{1,0:T(8,128)(2,1)} %all-gather.2.cloned.1.call-done), kind=kOutput, calls=%fused_computation.3 | convolution fusion | flops 5637144576 | bytes 15990784 | tf_op jit(solution)/shard_map/dot_general | solution.py:118
  94.9 1.2 slice.205
  96.2 0.5 copy-done.1
  96.6 0.6 add_rsqrt_fusion
  97.5 0.4 copy-done.5
  97.9 2.0 mul.275.clone
  99.9 3.1 %mul.283 = f32[16,64,256]{2,1,0:T(8,128)} reshape(f32[1024,2,128]{2,1,0:T(2,128)} %mul.275.clone) | data formatting | bytes 2097152 | tf_op jit(solution)/shard_map/mul | solution.py:31
  103.0 1.3 copy.69
  104.3 1.1 convert_element_type.88
  105.5 1.3 copy.67
  106.8 2.1 squeeze.31
  108.9 1.0 fusion.124
  110.1 1.5 stack.7
  111.6 5.0 %all-to-all-start = ((bf16[8,1,2,256,256]{3,4,2,1,0:T(8,128)(2,1)}), bf16[8,1,2,256,256]{3,4,2,1,0:T(8,128)(2,1)}, u32[]{:S(2)}, u32[]{:S(2)}) async-start(bf16[8,1,2,256,256]{3,4,2,1,0:T(8,128)(2,1)} %stack.7), calls=%async_computation | async-start | bytes 4194304 | tf_op jit(solution)/shard_map/all_to_all | solution.py:86
  116.5 1.5 fusion.169
  123.1 0.8 fusion.168
  123.9 1.3 and_and_fusion
  125.2 1.2 and_and_fusion.2
  126.4 1.3 and_and_fusion.4
  127.7 1.3 and_and_fusion.6
  129.0 1.4 multiply_convert_fusion
  130.4 5.8 %multiply_reduce_fusion = (f32[2,1024]{1,0:T(2,128)S(1)}, f32[2,1024,1024]{1,2,0:T(8,128)}) fusion(bf16[1024,2,128]{0,2,1:T(8,128)(2,1)S(1)} %multiply_convert_fusion, f32[2,128]{1,0:T(2,128)S(1)} %bitcast.364, f32[1024,2]{0,1:T(2,128)S(1)} %copy-done.6, f32[1024,3,2,128]{0,3,2,1:T(8,128)} %copy-done.1), kind=kOutput, calls=%fused_computation.1 | convolution fusion | flops 541849600 | bytes 9978880 | tf_op jit(solution)/shard_map/qhd,khd->hqk/dot_general | solution.py:48
  136.2 9.9 %all-to-all-done = bf16[8,1,2,256,256]{3,4,2,1,0:T(8,128)(2,1)} async-done(((bf16[8,1,2,256,256]{3,4,2,1,0:T(8,128)(2,1)}), bf16[8,1,2,256,256]{3,4,2,1,0:T(8,128)(2,1)}, u32[]{:S(2)}, u32[]{:S(2)}) %all-to-all-start) | async-done | bytes 2097184 | tf_op jit(solution)/shard_map/all_to_all | solution.py:86
  146.2 1.7 fusion.202
  147.9 0.5 fusion.15
  148.4 0.5 fusion.14
  149.0 0.5 fusion.13
  149.5 0.5 fusion.12
  150.0 0.5 fusion.11
  150.5 0.5 fusion.10
  151.1 0.5 fusion.9
  151.6 0.5 fusion.8
  152.2 0.6 fusion.30
  152.8 0.6 fusion.28
  153.5 0.6 fusion.26
  154.1 0.6 fusion.24
  154.8 0.6 fusion.22
  155.4 0.6 fusion.20
  156.0 0.6 fusion.18
  156.7 0.6 fusion.16
  157.3 1.6 fusion.2
  159.2 1.8 fusion.54
  161.0 0.7 fusion.50
  161.8 0.7 fusion.48
  162.5 0.7 fusion.46
  163.2 0.7 fusion.44
  164.0 0.7 fusion.42
  164.7 0.7 fusion.40
  165.5 0.7 fusion.38
  166.2 0.7 fusion.57
  167.0 5.1 %convolution_convert_fusion = bf16[1024,3584]{1,0:T(8,128)(2,1)} fusion(bf16[1024,256]{0,1:T(8,128)(2,1)S(1)} %bitcast.342, bf16[256,3584]{1,0:T(8,128)(2,1)S(1)} %copy-done), kind=kOutput, calls=%fused_computation.2 | convolution fusion | flops 1882718208 | bytes 9699328 | tf_op jit(solution)/shard_map/dot_general | solution.py:102
  172.1 92.5 %reduce-scatter.2.cloned.1.call-done = bf16[64,3584]{1,0:T(8,128)(2,1)} async-done(((bf16[1024,3584]{1,0:T(8,128)(2,1)}), bf16[64,3584]{1,0:T(8,128)(2,1)}) %reduce-scatter.2.cloned.1.call-update) | async-done | bytes 458768 | tf_op jit(solution)/shard_map/reduce_scatter | solution.py:124
  264.6 1.4 convolution_convert_fusion.1
  266.0 2.5 collective-permute-start
  268.5 1.9 fusion.126
  270.6 1.8 collective-permute-done
  272.6 0.8 fusion.127
  (83 shorter events, 1.6 us)
Async XLA Ops:
  7.2 159.8 %copy-start = (bf16[256,3584]{1,0:T(8,128)(2,1)S(1)}, bf16[256,3584]{1,0:T(8,128)(2,1)}, u32[]{:S(2)}) copy-start(bf16[256,3584]{1,0:T(8,128)(2,1)} %param.17) | copy-start | bytes 5505028
  7.2 77.7 %all-gather.2.cloned.1.call-start = ((), (), s32[]{:S(2)}) async-start(), calls=%async_computation.2 | async-start | bytes 7798784 | tf_op jit(solution)/shard_map/all_gather | solution.py:119
  14.0 8.3 %copy-start.27 = (f32[2,256]{1,0:T(2,128)S(1)}, f32[2,256]{1,0:T(2,128)}, u32[]{:S(2)}) copy-start(f32[2,256]{1,0:T(2,128)} %param.16) | copy-start | bytes 6148
  94.7 1.9 copy-start.1
  97.3 0.6 copy-start.5
  99.9 5.6 %slice-start.2 = ((f32[1024,3,2,128]{0,3,2,1:T(8,128)}), f32[1024,1,2,128]{0,3,2,1:T(8,128)S(1)}, s32[]{:S(2)}) async-start(f32[1024,3,2,128]{0,3,2,1:T(8,128)} %copy-done.1), calls=%async_computation.6 | async-start | bytes 2097152 | tf_op jit(solution)/shard_map/slice | solution.py:70
  105.5 4.4 %slice-start.3 = ((bf16[16,64,256]{2,1,0:T(8,128)(2,1)}), bf16[16,16,256]{2,1,0:T(8,128)(2,1)S(1)}, s32[]{:S(2)}) async-start(bf16[16,64,256]{2,1,0:T(8,128)(2,1)} %convert_element_type.88), calls=%async_computation.7 | async-start | bytes 262144 | tf_op jit(solution)/shard_map/slice | solution.py:80
  106.8 2.1 copy-start.9
  111.6 11.5 %copy-start.28 = (s32[8]{0:T(128)S(1)}, s32[8]{0:T(128)}, u32[]{:S(2)}) copy-start(s32[8]{0:T(128)} %param.13) | copy-start | bytes 100
  111.6 17.5 %copy-start.8 = (f32[1024,2]{0,1:T(2,128)S(1)}, f32[1024,2]{0,1:T(2,128)}, u32[]{:S(2)}) copy-start(f32[1024,2]{0,1:T(2,128)} %get-tuple-element.81) | copy-start | bytes 24580
  111.6 17.5 %copy-start.26 = (f32[1,256]{1,0:T(1,128)S(1)}, f32[1,256]{1,0:T(1,128)}, u32[]{:S(2)}) copy-start(f32[1,256]{1,0:T(1,128)} %get-tuple-element.61) | copy-start | bytes 3076
  111.6 18.8 %copy-start.6 = (f32[1024,2]{0,1:T(2,128)S(1)}, f32[1024,2]{0,1:T(2,128)}, u32[]{:S(2)}) copy-start(f32[1024,2]{0,1:T(2,128)} %copy-done.5) | copy-start | bytes 24580
  111.6 34.6 %all-to-all-start = ((bf16[8,1,2,256,256]{3,4,2,1,0:T(8,128)(2,1)}), bf16[8,1,2,256,256]{3,4,2,1,0:T(8,128)(2,1)}, u32[]{:S(2)}, u32[]{:S(2)}) async-start(bf16[8,1,2,256,256]{3,4,2,1,0:T(8,128)(2,1)} %stack.7), calls=%async_computation | async-start | bytes 4194304 | tf_op jit(solution)/shard_map/all_to_all | solution.py:86
  116.5 148.1 %reduce-scatter.2.cloned.1.call-start = ((), (), s32[]{:S(2)}) async-start(), calls=%async_computation.3 | async-start | bytes 7798784 | tf_op jit(solution)/shard_map/reduce_scatter | solution.py:124
  125.2 27.0 %copy-start.10 = (pred[256]{0:T(512)(128)(4,1)}, pred[256]{0:T(512)(128)(4,1)S(1)}, u32[]{:S(2)}) copy-start(pred[256]{0:T(512)(128)(4,1)S(1)} %get-tuple-element.82) | copy-start | bytes 772
  125.2 27.7 %copy-start.12 = (pred[256]{0:T(512)(128)(4,1)}, pred[256]{0:T(512)(128)(4,1)S(1)}, u32[]{:S(2)}) copy-start(pred[256]{0:T(512)(128)(4,1)S(1)} %get-tuple-element.83) | copy-start | bytes 772
  126.4 27.0 %copy-start.14 = (pred[256]{0:T(512)(128)(4,1)}, pred[256]{0:T(512)(128)(4,1)S(1)}, u32[]{:S(2)}) copy-start(pred[256]{0:T(512)(128)(4,1)S(1)} %get-tuple-element.84) | copy-start | bytes 772
  126.4 27.7 %copy-start.16 = (pred[256]{0:T(512)(128)(4,1)}, pred[256]{0:T(512)(128)(4,1)S(1)}, u32[]{:S(2)}) copy-start(pred[256]{0:T(512)(128)(4,1)S(1)} %get-tuple-element.85) | copy-start | bytes 772
  127.7 22.3 %copy-start.18 = (pred[256]{0:T(512)(128)(4,1)}, pred[256]{0:T(512)(128)(4,1)S(1)}, u32[]{:S(2)}) copy-start(pred[256]{0:T(512)(128)(4,1)S(1)} %get-tuple-element.86) | copy-start | bytes 772
  127.7 22.8 %copy-start.20 = (pred[256]{0:T(512)(128)(4,1)}, pred[256]{0:T(512)(128)(4,1)S(1)}, u32[]{:S(2)}) copy-start(pred[256]{0:T(512)(128)(4,1)S(1)} %get-tuple-element.87) | copy-start | bytes 772
  129.0 22.1 %copy-start.22 = (pred[256]{0:T(512)(128)(4,1)}, pred[256]{0:T(512)(128)(4,1)S(1)}, u32[]{:S(2)}) copy-start(pred[256]{0:T(512)(128)(4,1)S(1)} %get-tuple-element.88) | copy-start | bytes 772
  129.0 22.6 %copy-start.24 = (pred[256]{0:T(512)(128)(4,1)}, pred[256]{0:T(512)(128)(4,1)S(1)}, u32[]{:S(2)}) copy-start(pred[256]{0:T(512)(128)(4,1)S(1)} %get-tuple-element.89) | copy-start | bytes 772
  152.2 5.1 %slice-start = ((s8[8388608]{0:T(1024)(128)(4,1)}), s8[4194304]{0:T(1024)(128)(4,1)S(1)}, s32[]{:S(2)}) async-start(s8[8388608]{0:T(1024)(128)(4,1)} %bitcast.339), calls=%async_computation.4 | async-start | bytes 8388608
  153.5 1.3 copy-start.19
  154.1 1.3 copy-start.21
  154.8 1.3 copy-start.23
  154.8 2.5 slice-start.1
  155.4 1.3 copy-start.25
  157.3 1.9 copy-start.2
  163.2 0.7 copy-start.17
  164.0 0.7 copy-start.15
  164.7 0.7 copy-start.13
  165.5 0.7 copy-start.11
  172.1 92.6 %copy-start.3 = (bf16[1,64,3584]{2,1,0:T(8,128)(2,1)S(1)}, bf16[1,64,3584]{2,1,0:T(8,128)(2,1)}, u32[]{:S(2)}) copy-start(bf16[1,64,3584]{2,1,0:T(8,128)(2,1)} %param.10) | copy-start | bytes 1376260
  172.1 92.6 %copy-start.4 = (bf16[3584,96]{0,1:T(8,128)(2,1)S(1)}, bf16[3584,96]{0,1:T(8,128)(2,1)}, u32[]{:S(2)}) copy-start(bf16[3584,96]{0,1:T(8,128)(2,1)} %param.18) | copy-start | bytes 2064388
  172.1 98.4 %copy-start.7 = (bf16[3,96,384]{2,1,0:T(8,128)(2,1)S(1)}, bf16[3,96,384]{2,1,0:T(8,128)(2,1)}, u32[]{:S(2)}) copy-start(bf16[3,96,384]{2,1,0:T(8,128)(2,1)} %param.19) | copy-start | bytes 663556
  266.0 6.4 %collective-permute-start = (bf16[2,8,96]{2,1,0:T(8,128)(2,1)S(1)}, bf16[2,8,96]{2,1,0:T(8,128)(2,1)S(1)}, u32[]{:S(2)}, u32[]{:S(2)}) collective-permute-start(bf16[2,8,96]{2,1,0:T(8,128)(2,1)S(1)} %slice_bitcast_fusion.1), channel_id=1, source_target_pairs={{0,16},{16,32},{32,48},{48,64},{64,80},{80,96},{96,112},{1,17},{17... | collective-permute-start | bytes 9224 | tf_op jit(solution)/shard_map/ppermute | solution.py:18
Sparse Core Ops, SparseCore 0:
  14.1 70.7 all-gather.1
  172.2 92.3 reduce-scatter.1
